TPU v7x, 32 devices: a whole 2x2x4 slice. The times are simulated.
32 devices in a mesh: grp: 2 (over x), kv: 16 (over z, y, core).
Axes of the slice: x: 2, y: 2, z: 4, core: 2. Of those that a mesh axis runs over, the one named last changes fastest.
Arguments:
- queries: bfloat16 [32, 8192], P(('grp', 'kv')), parts along dimension 0, may hold values from -40 to 40
- stored_keys: bfloat16 [65536, 1024], P(('grp', 'kv')), parts along dimension 0, may hold values from -4.5 to 4.5
- stored_values: bfloat16 [65536, 1024], P(('grp', 'kv')), parts along dimension 0, may hold values from -6 to 6
- kv_counts: int32 [32], P(('grp', 'kv')), parts along dimension 0, may hold values from 1 to 2048, 20480 in all
Outputs:
- attended: bfloat16 [32, 8192], P(('grp', 'kv')), parts along dimension 0
There are 2 independent parts, one for each index of `grp`. A program takes and returns all parts, laid end to end along the dimension named above; each array names one. Nothing has to cross between parts.
Inputs may be any that keep to these rules, and one draw needn't show every extreme that they name: `kv_counts`: every shard has a live slot; the fullest shard has all 2048 slots live; the counts sum to 16 * 2048 * 5 // 8.
All inputs are finite; a program needn't handle non-finite values.
Results may differ from a plain program's by a relative error of at most 0.0085.
Values may be sent and summed in bfloat16 or wider, within the bound.
A program may use at most 64 MiB of HBM per device.

v0:
```python
import functools
import math

import jax
import jax.numpy as jnp
from jax import lax
from jax.experimental import pallas as pl
from jax.experimental.pallas import tpu as pltpu
from jax.sharding import PartitionSpec as P

QUERY_HEADS = 64
KEY_VALUE_HEADS = 8
HEAD_DIM = 128
RATIO = QUERY_HEADS // KEY_VALUE_HEADS
FIRST = (0, 2, 6)
SIZE = (2, 4, 2)
PAIRS = len(SIZE)
TILE = 512
SCALE2 = HEAD_DIM ** (-0.5) * math.log2(math.e)
MESH = pl.DeviceIdType.MESH


def kernel(n, count_ref, q_hbm, k_hbm, v_hbm, out_ref,
           q_flat, q_rows, q_own, out_rows, k_buf, v_buf, q_buf,
           send_part, send_stat, pair_part, pair_stat,
           out_part, out_stat, out_row, recv_part, recv_row, s_buf,
           in_sem, k_sem, v_sem, q_send, q_recv, f_send, f_recv,
           x_send, x_recv, y_send, y_recv, p_send, p_recv, s_send, s_recv):
    me = lax.axis_index("kv")
    core = lax.rem(me, 2)
    chip = lax.div(me, 2)
    chips = n // 2
    sibling = me + 1 - 2 * core
    slots = k_buf.shape[1]
    block = min(chips, 8)

    def fetch(k):
        copies = []
        for g in range(FIRST[k], FIRST[k] + SIZE[k]):
            columns = pl.ds(g * HEAD_DIM, HEAD_DIM)
            copies.append(pltpu.make_async_copy(k_hbm.at[:, columns], k_buf.at[g], k_sem.at[g]))
            copies.append(pltpu.make_async_copy(v_hbm.at[:, columns], v_buf.at[g], v_sem.at[g]))
        return copies

    def rows(k):
        return pl.ds(FIRST[k] * RATIO, SIZE[k] * RATIO)

    def to(device, src, dst, send, recv):
        return pltpu.make_async_remote_copy(
            src_ref=src, dst_ref=dst, send_sem=send, recv_sem=recv,
            device_id={"kv": device}, device_id_type=MESH)

    def each_chip(body):
        def step(d, carry):
            other = lax.rem(chip + d, chips)
            body(other, 2 * other + core)
            return carry
        lax.fori_loop(1, chips, step, 0)

    def blocks(body):
        if chips == block:
            body(0)
        else:
            def step(b, carry):
                body(b)
                return carry
            lax.fori_loop(0, chips // block, step, 0)

    q_in = pltpu.make_async_copy(q_hbm, q_flat, in_sem.at[0])
    q_in.start()
    barrier = pltpu.get_barrier_semaphore()

    def signal(device):
        pl.semaphore_signal(barrier, inc=1, device_id={"kv": device}, device_id_type=MESH)

    each_chip(lambda other, device: signal(device))
    signal(sibling)
    for k in range(PAIRS):
        for copy in fetch(k):
            copy.start()

    q_in.wait()
    for h in range(QUERY_HEADS):
        q_rows[h:h + 1, :] = q_flat[:, h * HEAD_DIM:(h + 1) * HEAD_DIM].astype(jnp.float32)
    own = q_rows[...].astype(jnp.bfloat16)
    q_own[...] = own
    q_buf[core, chip] = own
    live = lax.broadcasted_iota(jnp.int32, (1, slots), 1) < count_ref[0]
    out_stat[...] = jnp.zeros_like(out_stat)
    pl.semaphore_wait(barrier, chips)

    for k in range(PAIRS):
        each_chip(lambda other, device: to(
            device, q_own.at[rows(k)], q_buf.at[core, chip, rows(k)],
            q_send.at[k], q_recv.at[k]).start())

    def whole(buf, k, sem):
        part = buf.at[pl.ds(0, chips - 1), rows(k)]
        return pltpu.make_async_copy(part, part, sem.at[k])

    def forward(k):
        part = q_buf.at[core, :, rows(k)]
        return to(sibling, part, part, f_send.at[k], f_recv.at[k])

    def swap_part(k):
        return to(sibling, send_part.at[1 - core, :, rows(k)], pair_part.at[:, rows(k)],
                  x_send.at[k], x_recv.at[k])

    def swap_stat(k):
        return to(sibling, send_stat.at[1 - core, :, rows(k)], pair_stat.at[:, rows(k)],
                  y_send.at[k], y_recv.at[k])

    def take(k):
        whole(q_buf.at[core], k, q_recv).wait()
        forward(k).start()

    count = 2 * block * RATIO

    def compute(k):
        def one(b):
            group = pl.ds(b * block, block)
            parts = []
            stats = []
            peaks = []
            for half in range(SIZE[k]):
                g = FIRST[k] + half
                q = q_buf[:, group, g * RATIO:(g + 1) * RATIO, :].astype(jnp.float32)
                q = q.reshape(count, HEAD_DIM).astype(jnp.bfloat16)
                peak = jnp.full((count, HEAD_DIM), -1e30, jnp.float32)
                for c in range(0, slots, TILE):
                    s = lax.dot_general(q, k_buf[g, c:c + TILE], (((1,), (1,)), ((), ())),
                                        preferred_element_type=jnp.float32)
                    s = jnp.where(live[:, c:c + TILE], s, -1e30)
                    s_buf[half, :, c:c + TILE] = s
                    for d in range(0, TILE, HEAD_DIM):
                        peak = jnp.maximum(peak, s[:, d:d + HEAD_DIM])
                peaks.append(jnp.max(peak, axis=1, keepdims=True) * SCALE2)
            for half in range(SIZE[k]):
                g = FIRST[k] + half
                top = peaks[half]
                total = jnp.zeros((count, HEAD_DIM), jnp.float32)
                o = jnp.zeros((count, HEAD_DIM), jnp.float32)
                for c in range(0, slots, TILE):
                    p = jnp.exp2(s_buf[half, :, c:c + TILE] * SCALE2 - top)
                    for d in range(0, TILE, HEAD_DIM):
                        total = total + p[:, d:d + HEAD_DIM]
                    o = o + jnp.dot(p.astype(jnp.bfloat16), v_buf[g, c:c + TILE],
                                    preferred_element_type=jnp.float32)
                total = jnp.broadcast_to(jnp.sum(total, axis=1, keepdims=True), o.shape)
                parts.append((o / total).reshape(2, block, RATIO, HEAD_DIM))
                stats.append((top + jnp.log2(total)).reshape(2, block, RATIO, HEAD_DIM))
            send_part[:, group, rows(k), :] = jnp.concatenate(parts, axis=2).astype(jnp.bfloat16)
            send_stat[:, group, rows(k), :] = jnp.concatenate(stats, axis=2)

        blocks(one)
        swap_part(k).start()
        swap_stat(k).start()

    shape = (block, RATIO, HEAD_DIM)
    lane = lax.broadcasted_iota(jnp.int32, shape, 2)
    row = lax.broadcasted_iota(jnp.int32, shape, 1)

    def merge(k):
        swap_part(k).wait_recv()
        swap_stat(k).wait_recv()

        def one(b):
            group = pl.ds(b * block, block)
            a = send_part[core, group, rows(k), :].astype(jnp.float32)
            c = pair_part[group, rows(k), :].astype(jnp.float32)
            la = send_stat[core, group, rows(k), :]
            lc = pair_stat[group, rows(k), :]
            top = jnp.maximum(la, lc)
            wa = jnp.exp2(la - top)
            wc = jnp.exp2(lc - top)
            total = wa + wc
            out_part[group, rows(k), :] = ((wa * a + wc * c) / total).astype(jnp.bfloat16)
            lse = top + jnp.log2(total)
            stat = out_stat[group]
            for half in range(SIZE[k]):
                g = FIRST[k] + half
                stat = jnp.where(lane == g * RATIO + row, lse[:, half * RATIO:(half + 1) * RATIO, :], stat)
            if k < PAIRS - 1:
                out_stat[group] = stat
            else:
                out_row[group] = jnp.sum(stat, axis=1, keepdims=True)

        blocks(one)
        each_chip(lambda other, device: to(
            device, out_part.at[other, rows(k)], recv_part.at[chip, rows(k)],
            p_send.at[k], p_recv.at[k]).start())
        if k == PAIRS - 1:
            each_chip(lambda other, device: to(
                device, out_row.at[other], recv_row.at[chip],
                s_send.at[0], s_recv.at[0]).start())

    take(0)
    take(1)
    for k in range(PAIRS):
        forward(k).wait_recv()
        for copy in fetch(k):
            copy.wait()
        compute(k)
        if k + 2 < PAIRS:
            take(k + 2)
        if k > 0:
            merge(k - 1)
    merge(PAIRS - 1)
    recv_part[chip] = out_part[chip]
    recv_row[chip] = out_row[chip]

    def row_bytes(sem):
        part = recv_row.at[pl.ds(0, chips - 1)]
        return pltpu.make_async_copy(part, part, sem.at[0])

    for k in range(PAIRS):
        whole(recv_part, k, p_recv).wait()
    row_bytes(s_recv).wait()

    lse = recv_row[...]
    weight = jnp.exp2(lse - jnp.max(lse, axis=0, keepdims=True))
    recv_row[...] = weight / jnp.sum(weight, axis=0, keepdims=True)
    lane2 = lax.broadcasted_iota(jnp.int32, (RATIO, HEAD_DIM), 1)
    row2 = lax.broadcasted_iota(jnp.int32, (RATIO, HEAD_DIM), 0)

    def add(j, acc):
        w = jnp.broadcast_to(recv_row[j], (RATIO, HEAD_DIM))
        x = recv_part[j].astype(jnp.float32)
        new = []
        for g in range(KEY_VALUE_HEADS):
            col = jnp.sum(jnp.where(lane2 == g * RATIO + row2, w, 0.0), axis=1, keepdims=True)
            new.append(acc[g] + col * x[g * RATIO:(g + 1) * RATIO, :])
        return tuple(new)

    zero = jnp.zeros((RATIO, HEAD_DIM), jnp.float32)
    acc = lax.fori_loop(0, chips, add, (zero,) * KEY_VALUE_HEADS, unroll=block)
    out_rows[...] = jnp.concatenate(acc, axis=0)
    for h in range(QUERY_HEADS):
        out_ref[:, h * HEAD_DIM:(h + 1) * HEAD_DIM] = out_rows[h:h + 1, :].astype(out_ref.dtype)

    for k in range(PAIRS):
        whole(q_buf.at[core], k, q_send).wait()
        whole(recv_part, k, p_send).wait()
        forward(k).wait_send()
        swap_part(k).wait_send()
        swap_stat(k).wait_send()
    row_bytes(s_send).wait()


def solution(mesh):
    n = mesh.shape["kv"]

    def body(queries, stored_keys, stored_values, kv_counts):
        slots = stored_keys.shape[0]
        chips = n // 2
        hbm = pl.BlockSpec(memory_space=pltpu.HBM)
        part = (chips, QUERY_HEADS, HEAD_DIM)
        both = (2,) + part
        dma = pltpu.SemaphoreType.DMA
        f32, b16 = jnp.float32, jnp.bfloat16
        return pl.pallas_call(
            functools.partial(kernel, n),
            out_shape=jax.ShapeDtypeStruct(queries.shape, b16),
            in_specs=[pl.BlockSpec(memory_space=pltpu.SMEM), hbm, hbm, hbm],
            out_specs=pl.BlockSpec(memory_space=pltpu.VMEM),
            scratch_shapes=[
                pltpu.VMEM(queries.shape, b16),
                pltpu.VMEM((QUERY_HEADS, HEAD_DIM), f32),
                pltpu.VMEM((QUERY_HEADS, HEAD_DIM), b16),
                pltpu.VMEM((QUERY_HEADS, HEAD_DIM), f32),
                pltpu.VMEM((KEY_VALUE_HEADS, slots, HEAD_DIM), b16),
                pltpu.VMEM((KEY_VALUE_HEADS, slots, HEAD_DIM), b16),
                pltpu.VMEM(both, b16),
                pltpu.VMEM(both, b16),
                pltpu.VMEM(both, f32),
                pltpu.VMEM(part, b16),
                pltpu.VMEM(part, f32),
                pltpu.VMEM(part, b16),
                pltpu.VMEM((chips, RATIO, HEAD_DIM), f32),
                pltpu.VMEM((chips, 1, HEAD_DIM), f32),
                pltpu.VMEM(part, b16),
                pltpu.VMEM((chips, 1, HEAD_DIM), f32),
                pltpu.VMEM((4, 2 * min(chips, 8) * RATIO, slots), f32),
                dma((1,)),
            ] + [dma((KEY_VALUE_HEADS,))] * 2 + [dma((PAIRS,))] * 10 + [dma((1,))] * 2,
            compiler_params=pltpu.CompilerParams(
                collective_id=0, has_side_effects=True, vmem_limit_bytes=62 << 20),
        )(kv_counts, queries, stored_keys, stored_values)

    return jax.shard_map(
        body,
        mesh=mesh,
        in_specs=(
            P(("grp", "kv"), None),
            P(("grp", "kv"), None),
            P(("grp", "kv"), None),
            P(("grp", "kv")),
        ),
        out_specs=P(("grp", "kv"), None),
        check_vma=False,
    )
```

profile of v0, /device:TPU:0, one launch (start us, length us, event | category | flops | bytes accessed | tf_op | source)
XLA Modules:
  0.0 23.9 jit_solution(13625327452261690312)
XLA Ops:
  0.7 21.8 %shard_map.46 = bf16[1,8192]{1,0:T(2,128)(2,1)} custom-call(s32[1]{0:T(128)S(6)} %copy.6.count_ref, bf16[1,8192]{1,0:T(2,128)(2,1)} %q_hbm.1, bf16[2048,1024]{1,0:T(8,128)(2,1)} %k_hbm.1, bf16[2048,1024]{1,0:T(8,128)(2,1)} %v_hbm.1), custom_call_target="tpu_custom_call" | custom-call | tf_op jit(solution)/shard_map/pallas_call | solution.py:261
  22.5 1.4 %copy.7 = bf16[1,8192]{1,0:T(2,128)(2,1)} copy(bf16[1,8192]{1,0:T(2,128)(2,1)} %shard_map.46) | data formatting | bytes 32768
where the time goes:
time: 24.1 us; the launch traced here: 23.9 us
  Pallas kernels  21.8 us (90%)
  local copies, waits for them, and re-layouts  1.41 us (6%)
  between operations  0.66 us (3%)
    pallas_call x1, Pallas kernels, body(): pl.pallas_call(functools.partial(kernel, n), out_shape=jax.ShapeDtypeStru...  21.8 us
    unnamed x1, local copies, waits for them, and re-layouts  1.41 us

commit v1 on v0

--- a/solution.py
+++ b/solution.py
@@ -284,8 +284,9 @@
                 dma((1,)),
             ] + [dma((KEY_VALUE_HEADS,))] * 2 + [dma((PAIRS,))] * 10 + [dma((1,))] * 2,
             compiler_params=pltpu.CompilerParams(
-                collective_id=0, has_side_effects=True, vmem_limit_bytes=62 << 20),
-        )(kv_counts, queries, stored_keys, stored_values)
+                collective_id=0, has_side_effects=True, vmem_limit_bytes=40 << 20),
+        )(kv_counts, *[pltpu.with_memory_space_constraint(x, pltpu.HBM)
+                       for x in (queries, stored_keys, stored_values)])
 
     return jax.shard_map(
         body,

time: 24.1 us -> 22.7 us (0.942)
  local copies, waits for them, and re-layouts: 1.41 us -> 0.62 us
  Pallas kernels: 21.8 us -> 21.2 us
    unnamed x1, local copies, waits for them, and re-layouts: 1.41 us -> 0.62 us
    pallas_call x1, Pallas kernels: 21.8 us -> 21.2 us  [body(): pl.pallas_call(functools.partial(kernel, n), out_shape=jax.ShapeDtypeStru...]
where the time goes in v1:
time: 22.7 us; the launch traced here: 22.5 us
  Pallas kernels  21.2 us (93%)
  between operations  0.66 us (3%)
  local copies, waits for them, and re-layouts  0.62 us (3%)
    pallas_call x1, Pallas kernels, body(): pl.pallas_call(functools.partial(kernel, n), out_shape=jax.ShapeDtypeStru...  21.2 us
    unnamed x1, local copies, waits for them, and re-layouts  0.62 us

profile of v1, /device:TPU:0, one launch (start us, length us, event | category | flops | bytes accessed | tf_op | source)
XLA Modules:
  0.0 22.5 jit_solution(6033570403861660189)
XLA Ops:
  0.7 21.2 %shard_map.46 = bf16[1,8192]{1,0:T(2,128)(2,1)S(1)} custom-call(s32[1]{0:T(128)S(6)} %copy.6.count_ref, bf16[1,8192]{1,0:T(2,128)(2,1)} %q_hbm.1, bf16[2048,1024]{1,0:T(8,128)(2,1)} %k_hbm.1, bf16[2048,1024]{1,0:T(8,128)(2,1)} %v_hbm.1), custom_call_target="tpu_custom_call" | custom-call | tf_op jit(solution)/shard_map/pallas_call | solution.py:261
  21.9 0.6 %copy.7 = bf16[1,8192]{1,0:T(2,128)(2,1)} copy(bf16[1,8192]{1,0:T(2,128)(2,1)S(1)} %shard_map.46) | data formatting | bytes 32768

commit v2 on v1

--- a/solution.py
+++ b/solution.py
@@ -16,13 +16,14 @@
 SIZE = (2, 4, 2)
 PAIRS = len(SIZE)
 TILE = 512
+FILL = 256
 SCALE2 = HEAD_DIM ** (-0.5) * math.log2(math.e)
 MESH = pl.DeviceIdType.MESH
 
 
 def kernel(n, count_ref, q_hbm, k_hbm, v_hbm, out_ref,
            q_flat, q_rows, q_own, out_rows, k_buf, v_buf, q_buf,
-           send_part, send_stat, pair_part, pair_stat,
+           live_buf, send_part, send_stat, pair_part, pair_stat,
            out_part, out_stat, out_row, recv_part, recv_row, s_buf,
            in_sem, k_sem, v_sem, q_send, q_recv, f_send, f_recv,
            x_send, x_recv, y_send, y_recv, p_send, p_recv, s_send, s_recv):
@@ -85,7 +86,9 @@
     own = q_rows[...].astype(jnp.bfloat16)
     q_own[...] = own
     q_buf[core, chip] = own
-    live = lax.broadcasted_iota(jnp.int32, (1, slots), 1) < count_ref[0]
+    limit = count_ref[0]
+    live = lax.broadcasted_iota(jnp.int32, (slots, HEAD_DIM), 0) < limit
+    live_buf[...] = jnp.where(live, 1.0, 0.0).astype(jnp.bfloat16)
     out_stat[...] = jnp.zeros_like(out_stat)
     pl.semaphore_wait(barrier, chips)
 
@@ -115,6 +118,21 @@
         forward(k).start()
 
     count = 2 * block * RATIO
+
+    def prepare(k):
+        for copy in fetch(k):
+            copy.wait()
+        for g in range(FIRST[k], FIRST[k] + SIZE[k]):
+            spare = jnp.broadcast_to(k_buf[g, 0:1].astype(jnp.float32), (FILL, HEAD_DIM)).astype(jnp.bfloat16)
+
+            def step(i, carry):
+                part = pl.ds(pl.multiple_of(i * FILL, FILL), FILL)
+                keep = live_buf[part]
+                k_buf[g, part] = k_buf[g, part] * keep + spare * (1 - keep)
+                v_buf[g, part] = v_buf[g, part] * keep
+                return carry
+
+            lax.fori_loop(0, slots // FILL, step, 0)
 
     def compute(k):
         def one(b):
@@ -130,7 +148,6 @@
                 for c in range(0, slots, TILE):
                     s = lax.dot_general(q, k_buf[g, c:c + TILE], (((1,), (1,)), ((), ())),
                                         preferred_element_type=jnp.float32)
-                    s = jnp.where(live[:, c:c + TILE], s, -1e30)
                     s_buf[half, :, c:c + TILE] = s
                     for d in range(0, TILE, HEAD_DIM):
                         peak = jnp.maximum(peak, s[:, d:d + HEAD_DIM])
@@ -138,15 +155,13 @@
             for half in range(SIZE[k]):
                 g = FIRST[k] + half
                 top = peaks[half]
-                total = jnp.zeros((count, HEAD_DIM), jnp.float32)
-                o = jnp.zeros((count, HEAD_DIM), jnp.float32)
+                o = jnp.zeros((count, 2 * HEAD_DIM), jnp.float32)
                 for c in range(0, slots, TILE):
                     p = jnp.exp2(s_buf[half, :, c:c + TILE] * SCALE2 - top)
-                    for d in range(0, TILE, HEAD_DIM):
-                        total = total + p[:, d:d + HEAD_DIM]
-                    o = o + jnp.dot(p.astype(jnp.bfloat16), v_buf[g, c:c + TILE],
-                                    preferred_element_type=jnp.float32)
-                total = jnp.broadcast_to(jnp.sum(total, axis=1, keepdims=True), o.shape)
+                    both = jnp.concatenate([v_buf[g, c:c + TILE], live_buf[c:c + TILE]], axis=1)
+                    o = o + jnp.dot(p.astype(jnp.bfloat16), both, preferred_element_type=jnp.float32)
+                total = o[:, HEAD_DIM:]
+                o = o[:, :HEAD_DIM]
                 parts.append((o / total).reshape(2, block, RATIO, HEAD_DIM))
                 stats.append((top + jnp.log2(total)).reshape(2, block, RATIO, HEAD_DIM))
             send_part[:, group, rows(k), :] = jnp.concatenate(parts, axis=2).astype(jnp.bfloat16)
@@ -194,12 +209,12 @@
                 device, out_row.at[other], recv_row.at[chip],
                 s_send.at[0], s_recv.at[0]).start())
 
+    for k in range(PAIRS):
+        prepare(k)
     take(0)
     take(1)
     for k in range(PAIRS):
         forward(k).wait_recv()
-        for copy in fetch(k):
-            copy.wait()
         compute(k)
         if k + 2 < PAIRS:
             take(k + 2)
@@ -271,6 +286,7 @@
                 pltpu.VMEM((KEY_VALUE_HEADS, slots, HEAD_DIM), b16),
                 pltpu.VMEM((KEY_VALUE_HEADS, slots, HEAD_DIM), b16),
                 pltpu.VMEM(both, b16),
+                pltpu.VMEM((slots, HEAD_DIM), b16),
                 pltpu.VMEM(both, b16),
                 pltpu.VMEM(both, f32),
                 pltpu.VMEM(part, b16),

time: 22.7 us -> 22.1 us (0.974)
  Pallas kernels: 21.2 us -> 20.7 us
    pallas_call x1, Pallas kernels: 21.2 us -> 20.7 us  [body(): pl.pallas_call(functools.partial(kernel, n), out_shape=jax.ShapeDtypeStru...]
where the time goes in v2:
time: 22.1 us; the launch traced here: 21.9 us
  Pallas kernels  20.7 us (94%)
  between operations  0.66 us (3%)
  local copies, waits for them, and re-layouts  0.62 us (3%)
    pallas_call x1, Pallas kernels, body(): pl.pallas_call(functools.partial(kernel, n), out_shape=jax.ShapeDtypeStru...  20.7 us
    unnamed x1, local copies, waits for them, and re-layouts  0.62 us

profile of v2, /device:TPU:0, one launch (start us, length us, event | category | flops | bytes accessed | tf_op | source)
XLA Modules:
  0.0 21.9 jit_solution(7924596385783590114)
XLA Ops:
  0.7 20.7 %shard_map.46 = bf16[1,8192]{1,0:T(2,128)(2,1)S(1)} custom-call(s32[1]{0:T(128)S(6)} %copy.6.count_ref, bf16[1,8192]{1,0:T(2,128)(2,1)} %q_hbm.1, bf16[2048,1024]{1,0:T(8,128)(2,1)} %k_hbm.1, bf16[2048,1024]{1,0:T(8,128)(2,1)} %v_hbm.1), custom_call_target="tpu_custom_call" | custom-call | tf_op jit(solution)/shard_map/pallas_call | solution.py:276
  21.3 0.6 %copy.7 = bf16[1,8192]{1,0:T(2,128)(2,1)} copy(bf16[1,8192]{1,0:T(2,128)(2,1)S(1)} %shard_map.46) | data formatting | bytes 32768

commit v3 on v1

--- a/solution.py
+++ b/solution.py
@@ -24,8 +24,7 @@
            q_flat, q_rows, q_own, out_rows, k_buf, v_buf, q_buf,
            send_part, send_stat, pair_part, pair_stat,
            out_part, out_stat, out_row, recv_part, recv_row, s_buf,
-           in_sem, k_sem, v_sem, q_send, q_recv, f_send, f_recv,
-           x_send, x_recv, y_send, y_recv, p_send, p_recv, s_send, s_recv):
+           in_sem, kv_sem, q_recv, f_recv, x_recv, p_recv, s_recv, sent):
     me = lax.axis_index("kv")
     core = lax.rem(me, 2)
     chip = lax.div(me, 2)
@@ -38,8 +37,8 @@
         copies = []
         for g in range(FIRST[k], FIRST[k] + SIZE[k]):
             columns = pl.ds(g * HEAD_DIM, HEAD_DIM)
-            copies.append(pltpu.make_async_copy(k_hbm.at[:, columns], k_buf.at[g], k_sem.at[g]))
-            copies.append(pltpu.make_async_copy(v_hbm.at[:, columns], v_buf.at[g], v_sem.at[g]))
+            copies.append(pltpu.make_async_copy(k_hbm.at[:, columns], k_buf.at[g], kv_sem.at[k]))
+            copies.append(pltpu.make_async_copy(v_hbm.at[:, columns], v_buf.at[g], kv_sem.at[k]))
         return copies
 
     def rows(k):
@@ -92,26 +91,25 @@
     for k in range(PAIRS):
         each_chip(lambda other, device: to(
             device, q_own.at[rows(k)], q_buf.at[core, chip, rows(k)],
-            q_send.at[k], q_recv.at[k]).start())
-
-    def whole(buf, k, sem):
-        part = buf.at[pl.ds(0, chips - 1), rows(k)]
-        return pltpu.make_async_copy(part, part, sem.at[k])
+            sent.at[0], q_recv.at[k]).start())
+
+    def amount(part, sem):
+        return pltpu.make_async_copy(part, part, sem)
 
     def forward(k):
         part = q_buf.at[core, :, rows(k)]
-        return to(sibling, part, part, f_send.at[k], f_recv.at[k])
+        return to(sibling, part, part, sent.at[0], f_recv.at[k])
 
     def swap_part(k):
         return to(sibling, send_part.at[1 - core, :, rows(k)], pair_part.at[:, rows(k)],
-                  x_send.at[k], x_recv.at[k])
+                  sent.at[0], x_recv.at[k])
 
     def swap_stat(k):
         return to(sibling, send_stat.at[1 - core, :, rows(k)], pair_stat.at[:, rows(k)],
-                  y_send.at[k], y_recv.at[k])
+                  sent.at[0], x_recv.at[k])
 
     def take(k):
-        whole(q_buf.at[core], k, q_recv).wait()
+        amount(q_buf.at[core, pl.ds(0, chips - 1), rows(k)], q_recv.at[k]).wait()
         forward(k).start()
 
     count = 2 * block * RATIO
@@ -122,6 +120,7 @@
             parts = []
             stats = []
             peaks = []
+            ones = jnp.ones((TILE, HEAD_DIM), jnp.bfloat16)
             for half in range(SIZE[k]):
                 g = FIRST[k] + half
                 q = q_buf[:, group, g * RATIO:(g + 1) * RATIO, :].astype(jnp.float32)
@@ -138,15 +137,13 @@
             for half in range(SIZE[k]):
                 g = FIRST[k] + half
                 top = peaks[half]
-                total = jnp.zeros((count, HEAD_DIM), jnp.float32)
-                o = jnp.zeros((count, HEAD_DIM), jnp.float32)
+                o = jnp.zeros((count, 2 * HEAD_DIM), jnp.float32)
                 for c in range(0, slots, TILE):
                     p = jnp.exp2(s_buf[half, :, c:c + TILE] * SCALE2 - top)
-                    for d in range(0, TILE, HEAD_DIM):
-                        total = total + p[:, d:d + HEAD_DIM]
-                    o = o + jnp.dot(p.astype(jnp.bfloat16), v_buf[g, c:c + TILE],
-                                    preferred_element_type=jnp.float32)
-                total = jnp.broadcast_to(jnp.sum(total, axis=1, keepdims=True), o.shape)
+                    both = jnp.concatenate([v_buf[g, c:c + TILE], ones], axis=1)
+                    o = o + jnp.dot(p.astype(jnp.bfloat16), both, preferred_element_type=jnp.float32)
+                total = o[:, HEAD_DIM:]
+                o = o[:, :HEAD_DIM]
                 parts.append((o / total).reshape(2, block, RATIO, HEAD_DIM))
                 stats.append((top + jnp.log2(total)).reshape(2, block, RATIO, HEAD_DIM))
             send_part[:, group, rows(k), :] = jnp.concatenate(parts, axis=2).astype(jnp.bfloat16)
@@ -161,8 +158,7 @@
     row = lax.broadcasted_iota(jnp.int32, shape, 1)
 
     def merge(k):
-        swap_part(k).wait_recv()
-        swap_stat(k).wait_recv()
+        amount(send_stat.at[0, :, pl.ds(0, 3 * SIZE[k] * RATIO // 2)], x_recv.at[k]).wait()
 
         def one(b):
             group = pl.ds(b * block, block)
@@ -188,18 +184,17 @@
         blocks(one)
         each_chip(lambda other, device: to(
             device, out_part.at[other, rows(k)], recv_part.at[chip, rows(k)],
-            p_send.at[k], p_recv.at[k]).start())
+            sent.at[0], p_recv.at[0]).start())
         if k == PAIRS - 1:
             each_chip(lambda other, device: to(
                 device, out_row.at[other], recv_row.at[chip],
-                s_send.at[0], s_recv.at[0]).start())
+                sent.at[0], s_recv.at[0]).start())
 
     take(0)
     take(1)
     for k in range(PAIRS):
         forward(k).wait_recv()
-        for copy in fetch(k):
-            copy.wait()
+        amount(k_buf.at[pl.ds(0, 2 * SIZE[k])], kv_sem.at[k]).wait()
         compute(k)
         if k + 2 < PAIRS:
             take(k + 2)
@@ -209,13 +204,9 @@
     recv_part[chip] = out_part[chip]
     recv_row[chip] = out_row[chip]
 
-    def row_bytes(sem):
-        part = recv_row.at[pl.ds(0, chips - 1)]
-        return pltpu.make_async_copy(part, part, sem.at[0])
-
-    for k in range(PAIRS):
-        whole(recv_part, k, p_recv).wait()
-    row_bytes(s_recv).wait()
+    others = pl.ds(0, chips - 1)
+    amount(recv_part.at[others], p_recv.at[0]).wait()
+    amount(recv_row.at[others], s_recv.at[0]).wait()
 
     lse = recv_row[...]
     weight = jnp.exp2(lse - jnp.max(lse, axis=0, keepdims=True))
@@ -238,13 +229,12 @@
     for h in range(QUERY_HEADS):
         out_ref[:, h * HEAD_DIM:(h + 1) * HEAD_DIM] = out_rows[h:h + 1, :].astype(out_ref.dtype)
 
-    for k in range(PAIRS):
-        whole(q_buf.at[core], k, q_send).wait()
-        whole(recv_part, k, p_send).wait()
-        forward(k).wait_send()
-        swap_part(k).wait_send()
-        swap_stat(k).wait_send()
-    row_bytes(s_send).wait()
+    amount(q_buf.at[0, others], sent.at[0]).wait()
+    amount(q_buf.at[0], sent.at[0]).wait()
+    amount(send_part.at[0], sent.at[0]).wait()
+    amount(send_stat.at[0], sent.at[0]).wait()
+    amount(recv_part.at[others], sent.at[0]).wait()
+    amount(recv_row.at[others], sent.at[0]).wait()
 
 
 def solution(mesh):
@@ -282,7 +272,7 @@
                 pltpu.VMEM((chips, 1, HEAD_DIM), f32),
                 pltpu.VMEM((4, 2 * min(chips, 8) * RATIO, slots), f32),
                 dma((1,)),
-            ] + [dma((KEY_VALUE_HEADS,))] * 2 + [dma((PAIRS,))] * 10 + [dma((1,))] * 2,
+            ] + [dma((PAIRS,))] * 4 + [dma((1,))] * 3,
             compiler_params=pltpu.CompilerParams(
                 collective_id=0, has_side_effects=True, vmem_limit_bytes=40 << 20),
         )(kv_counts, *[pltpu.with_memory_space_constraint(x, pltpu.HBM)

time: 22.7 us -> 21.7 us (0.956)
  Pallas kernels: 21.2 us -> 20.3 us
    pallas_call x1, Pallas kernels: 21.2 us -> 20.3 us  [body(): pl.pallas_call(functools.partial(kernel, n), out_shape=jax.ShapeDtypeStru...]
where the time goes in v3:
time: 21.7 us; the launch traced here: 21.6 us
  Pallas kernels  20.3 us (94%)
  between operations  0.66 us (3%)
  local copies, waits for them, and re-layouts  0.62 us (3%)
    pallas_call x1, Pallas kernels, body(): pl.pallas_call(functools.partial(kernel, n), out_shape=jax.ShapeDtypeStru...  20.3 us
    unnamed x1, local copies, waits for them, and re-layouts  0.62 us

profile of v3, /device:TPU:0, one launch (start us, length us, event | category | flops | bytes accessed | tf_op | source)
XLA Modules:
  0.0 21.6 jit_solution(5518912480176235162)
XLA Ops:
  0.7 20.3 %shard_map.46 = bf16[1,8192]{1,0:T(2,128)(2,1)S(1)} custom-call(s32[1]{0:T(128)S(6)} %copy.6.count_ref, bf16[1,8192]{1,0:T(2,128)(2,1)} %q_hbm.1, bf16[2048,1024]{1,0:T(8,128)(2,1)} %k_hbm.1, bf16[2048,1024]{1,0:T(8,128)(2,1)} %v_hbm.1), custom_call_target="tpu_custom_call" | custom-call | tf_op jit(solution)/shard_map/pallas_call | solution.py:251
  21.0 0.6 %copy.7 = bf16[1,8192]{1,0:T(2,128)(2,1)} copy(bf16[1,8192]{1,0:T(2,128)(2,1)S(1)} %shard_map.46) | data formatting | bytes 32768

commit v4 on v3

--- a/solution.py
+++ b/solution.py
@@ -15,6 +15,7 @@
 FIRST = (0, 2, 6)
 SIZE = (2, 4, 2)
 PAIRS = len(SIZE)
+NEAR = 3
 TILE = 512
 SCALE2 = HEAD_DIM ** (-0.5) * math.log2(math.e)
 MESH = pl.DeviceIdType.MESH
@@ -24,7 +25,7 @@
            q_flat, q_rows, q_own, out_rows, k_buf, v_buf, q_buf,
            send_part, send_stat, pair_part, pair_stat,
            out_part, out_stat, out_row, recv_part, recv_row, s_buf,
-           in_sem, kv_sem, q_recv, f_recv, x_recv, p_recv, s_recv, sent):
+           far_sem, in_sem, kv_sem, z_recv, q_recv, f_recv, x_recv, p_recv, s_recv, sent):
     me = lax.axis_index("kv")
     core = lax.rem(me, 2)
     chip = lax.div(me, 2)
@@ -72,8 +73,35 @@
     def signal(device):
         pl.semaphore_signal(barrier, inc=1, device_id={"kv": device}, device_id_type=MESH)
 
-    each_chip(lambda other, device: signal(device))
+    end = chips - 1
+    near = chip < NEAR
+    last = chip == end
+
     signal(sibling)
+
+    @pl.when(near)
+    def _():
+        signal(2 * end + 1 - core)
+
+    @pl.when(jnp.logical_not(last))
+    def _():
+        each_chip(lambda other, device: signal(device))
+
+    @pl.when(last)
+    def _():
+        pl.semaphore_wait(barrier, chips + NEAR)
+
+        def greet(device):
+            pl.semaphore_signal(far_sem, inc=1, device_id={"kv": device}, device_id_type=MESH)
+
+        for device in range(2 * NEAR):
+            greet(jnp.int32(device))
+
+        def step(other, carry):
+            greet(2 * other + core)
+            return carry
+        lax.fori_loop(NEAR, end, step, 0)
+
     for k in range(PAIRS):
         for copy in fetch(k):
             copy.start()
@@ -86,19 +114,64 @@
     q_buf[core, chip] = own
     live = lax.broadcasted_iota(jnp.int32, (1, slots), 1) < count_ref[0]
     out_stat[...] = jnp.zeros_like(out_stat)
-    pl.semaphore_wait(barrier, chips)
-
-    for k in range(PAIRS):
-        each_chip(lambda other, device: to(
-            device, q_own.at[rows(k)], q_buf.at[core, chip, rows(k)],
-            sent.at[0], q_recv.at[k]).start())
+    def give(other, device, k, recv):
+        to(device, q_own.at[rows(k)], q_buf.at[core, chip, rows(k)], sent.at[0], recv.at[k]).start()
+
+    @pl.when(last)
+    def _():
+        for k in range(PAIRS):
+            each_chip(lambda other, device: give(other, device, k, q_recv))
+
+    @pl.when(jnp.logical_not(last))
+    def _():
+        pl.semaphore_wait(barrier, chips - 1)
+        for k in range(PAIRS):
+            def ahead(other, device):
+                @pl.when(other != end)
+                def _():
+                    give(other, device, k, q_recv)
+            each_chip(ahead)
+
+        @pl.when(near)
+        def _():
+            pl.semaphore_wait(far_sem, 2)
+            for k in range(PAIRS):
+                for to_core in range(2):
+                    give(end, 2 * end + to_core, k, z_recv)
+
+        @pl.when(chip >= NEAR)
+        def _():
+            pl.semaphore_wait(far_sem, 1)
+            for k in range(PAIRS):
+                give(end, 2 * end + core, k, q_recv)
 
     def amount(part, sem):
         return pltpu.make_async_copy(part, part, sem)
 
-    def forward(k):
-        part = q_buf.at[core, :, rows(k)]
+    def across(k, start):
+        part = q_buf.at[core, pl.ds(start, chips - start), rows(k)]
         return to(sibling, part, part, sent.at[0], f_recv.at[k])
+
+    def take(k):
+        @pl.when(last)
+        def _():
+            amount(q_buf.at[core, pl.ds(0, end - NEAR), rows(k)], q_recv.at[k]).wait()
+            across(k, NEAR).start()
+
+        @pl.when(jnp.logical_not(last))
+        def _():
+            amount(q_buf.at[core, pl.ds(0, chips - 1), rows(k)], q_recv.at[k]).wait()
+            across(k, 0).start()
+
+    def gathered(k):
+        @pl.when(last)
+        def _():
+            across(k, NEAR).wait_recv()
+            amount(q_buf.at[:, pl.ds(0, NEAR), rows(k)], z_recv.at[k]).wait()
+
+        @pl.when(jnp.logical_not(last))
+        def _():
+            across(k, 0).wait_recv()
 
     def swap_part(k):
         return to(sibling, send_part.at[1 - core, :, rows(k)], pair_part.at[:, rows(k)],
@@ -107,10 +180,6 @@
     def swap_stat(k):
         return to(sibling, send_stat.at[1 - core, :, rows(k)], pair_stat.at[:, rows(k)],
                   sent.at[0], x_recv.at[k])
-
-    def take(k):
-        amount(q_buf.at[core, pl.ds(0, chips - 1), rows(k)], q_recv.at[k]).wait()
-        forward(k).start()
 
     count = 2 * block * RATIO
 
@@ -193,7 +262,7 @@
     take(0)
     take(1)
     for k in range(PAIRS):
-        forward(k).wait_recv()
+        gathered(k)
         amount(k_buf.at[pl.ds(0, 2 * SIZE[k])], kv_sem.at[k]).wait()
         compute(k)
         if k + 2 < PAIRS:
@@ -230,7 +299,19 @@
         out_ref[:, h * HEAD_DIM:(h + 1) * HEAD_DIM] = out_rows[h:h + 1, :].astype(out_ref.dtype)
 
     amount(q_buf.at[0, others], sent.at[0]).wait()
-    amount(q_buf.at[0], sent.at[0]).wait()
+
+    @pl.when(last)
+    def _():
+        amount(q_buf.at[0, pl.ds(0, chips - NEAR)], sent.at[0]).wait()
+
+    @pl.when(jnp.logical_not(last))
+    def _():
+        amount(q_buf.at[0], sent.at[0]).wait()
+
+    @pl.when(near)
+    def _():
+        amount(q_buf.at[0, 0], sent.at[0]).wait()
+
     amount(send_part.at[0], sent.at[0]).wait()
     amount(send_stat.at[0], sent.at[0]).wait()
     amount(recv_part.at[others], sent.at[0]).wait()
@@ -271,8 +352,9 @@
                 pltpu.VMEM(part, b16),
                 pltpu.VMEM((chips, 1, HEAD_DIM), f32),
                 pltpu.VMEM((4, 2 * min(chips, 8) * RATIO, slots), f32),
+                pltpu.SemaphoreType.REGULAR,
                 dma((1,)),
-            ] + [dma((PAIRS,))] * 4 + [dma((1,))] * 3,
+            ] + [dma((PAIRS,))] * 5 + [dma((1,))] * 3,
             compiler_params=pltpu.CompilerParams(
                 collective_id=0, has_side_effects=True, vmem_limit_bytes=40 << 20),
         )(kv_counts, *[pltpu.with_memory_space_constraint(x, pltpu.HBM)

time: 21.7 us -> 21.1 us (0.972)
  Pallas kernels: 20.3 us -> 19.7 us
    pallas_call x1, Pallas kernels: 20.3 us -> 19.7 us  [body(): pl.pallas_call(functools.partial(kernel, n), out_shape=jax.ShapeDtypeStru...]
where the time goes in v4:
time: 21.1 us; the launch traced here: 21 us
  Pallas kernels  19.7 us (93%)
  between operations  0.66 us (3%)
  local copies, waits for them, and re-layouts  0.62 us (3%)
    pallas_call x1, Pallas kernels, body(): pl.pallas_call(functools.partial(kernel, n), out_shape=jax.ShapeDtypeStru...  19.7 us
    unnamed x1, local copies, waits for them, and re-layouts  0.62 us

profile of v4, /device:TPU:0, one launch (start us, length us, event | category | flops | bytes accessed | tf_op | source)
XLA Modules:
  0.0 21.0 jit_solution(3722206531632032761)
XLA Ops:
  0.7 19.7 %shard_map.46 = bf16[1,8192]{1,0:T(2,128)(2,1)S(1)} custom-call(s32[1]{0:T(128)S(6)} %copy.6.count_ref, bf16[1,8192]{1,0:T(2,128)(2,1)} %q_hbm.1, bf16[2048,1024]{1,0:T(8,128)(2,1)} %k_hbm.1, bf16[2048,1024]{1,0:T(8,128)(2,1)} %v_hbm.1), custom_call_target="tpu_custom_call" | custom-call | tf_op jit(solution)/shard_map/pallas_call | solution.py:332
  20.4 0.6 %copy.7 = bf16[1,8192]{1,0:T(2,128)(2,1)} copy(bf16[1,8192]{1,0:T(2,128)(2,1)S(1)} %shard_map.46) | data formatting | bytes 32768

commit v5 on v4

--- a/solution.py
+++ b/solution.py
@@ -251,13 +251,13 @@
                 out_row[group] = jnp.sum(stat, axis=1, keepdims=True)
 
         blocks(one)
-        each_chip(lambda other, device: to(
-            device, out_part.at[other, rows(k)], recv_part.at[chip, rows(k)],
-            sent.at[0], p_recv.at[0]).start())
-        if k == PAIRS - 1:
-            each_chip(lambda other, device: to(
-                device, out_row.at[other], recv_row.at[chip],
-                sent.at[0], s_recv.at[0]).start())
+        def deliver(other, device):
+            to(device, out_part.at[other, rows(k)], recv_part.at[chip, rows(k)],
+               sent.at[0], p_recv.at[0]).start()
+            if k == PAIRS - 1:
+                to(device, out_row.at[other], recv_row.at[chip], sent.at[0], s_recv.at[0]).start()
+
+        each_chip(deliver)
 
     take(0)
     take(1)

time: 21.1 us -> 21 us (level)
  no operation moved by 1% of the time
where the time goes in v5:
time: 21 us; the launch traced here: 20.9 us
  Pallas kernels  19.6 us (93%)
  between operations  0.66 us (3%)
  local copies, waits for them, and re-layouts  0.62 us (3%)
    pallas_call x1, Pallas kernels, body(): pl.pallas_call(functools.partial(kernel, n), out_shape=jax.ShapeDtypeStru...  19.6 us
    unnamed x1, local copies, waits for them, and re-layouts  0.62 us

profile of v5, /device:TPU:0, one launch (start us, length us, event | category | flops | bytes accessed | tf_op | source)
XLA Modules:
  0.0 20.9 jit_solution(9993823829869846997)
XLA Ops:
  0.7 19.6 %shard_map.46 = bf16[1,8192]{1,0:T(2,128)(2,1)S(1)} custom-call(s32[1]{0:T(128)S(6)} %copy.6.count_ref, bf16[1,8192]{1,0:T(2,128)(2,1)} %q_hbm.1, bf16[2048,1024]{1,0:T(8,128)(2,1)} %k_hbm.1, bf16[2048,1024]{1,0:T(8,128)(2,1)} %v_hbm.1), custom_call_target="tpu_custom_call" | custom-call | tf_op jit(solution)/shard_map/pallas_call | solution.py:332
  20.2 0.6 %copy.7 = bf16[1,8192]{1,0:T(2,128)(2,1)} copy(bf16[1,8192]{1,0:T(2,128)(2,1)S(1)} %shard_map.46) | data formatting | bytes 32768
